TPU v7x, 512 devices: a whole 4x4x16 slice. The times are simulated.
512 devices in a mesh: ctx: 64 (over x, y, z_hi, core), head: 8 (over z_lo).
Axes of the slice: x: 4, y: 4, z: 16 (z_hi: 2, z_lo: 8; z = z_hi * 8 + z_lo), core: 2. Of those that a mesh axis runs over, the one named last changes fastest.
Arguments:
- queries: bfloat16 [16384, 32, 128], P('ctx', 'head'), may hold values from -300 to 300
- keys: bfloat16 [16384, 8, 128], P('ctx', 'head'), may hold values from -12 to 12
- values: bfloat16 [16384, 8, 128], P('ctx', 'head'), may hold values from -150 to 150
- tangent_queries: bfloat16 [16384, 32, 128], P('ctx', 'head'), may hold values from -6 to 6
- tangent_keys: bfloat16 [16384, 8, 128], P('ctx', 'head'), may hold values from -6 to 6
- tangent_values: bfloat16 [16384, 8, 128], P('ctx', 'head'), may hold values from -6 to 6
- doc_start: int32 [128], P('ctx'), may hold values from 0 to 127, as said below
- out_gain: float32 [4096], P('head'), may hold values from 0.1 to 1.9
Outputs:
- product_queries: float32 [16384, 32, 128], P('ctx', 'head')
- product_keys: float32 [16384, 8, 128], P('ctx', 'head')
- product_values: float32 [16384, 8, 128], P('ctx', 'head')
Inputs may be any that keep to these rules, and one draw needn't show every extreme that they name: Documents are runs of whole mask blocks; doc_start[b] is the first block of b's document, so it never falls and doc_start[b] <= b. No document is longer than 16 blocks, and one is exactly 16 blocks long.
All inputs are finite; a program needn't handle non-finite values.
Results may differ from a plain program's by a relative error of at most 0.014.
Values may be sent and summed in bfloat16 or wider, within the bound.
A program may use at most 64 MiB of HBM per device.

v0:
```python
import jax
import jax.numpy as jnp
from jax import lax
from jax.sharding import PartitionSpec as P

QH = 32
HD = 128
DOC_DEVS = 8


EPSILON = 1e-06


def passed_along(value, axis, steps):
    count = lax.axis_size(axis)
    leading, last = (max(0, -steps), min(count, count - steps))
    return lax.ppermute(value, axis, [(source, source + steps) for source in range(leading, last)])


def from_behind(value, axis, steps):
    count = lax.axis_size(axis)
    pairs = [(source, (source + steps) % count) for source in range(count)]
    return lax.ppermute(value, axis, pairs)


def heads_first(array, key_heads):
    rows, query_heads, width = array.shape
    return array.reshape(rows, key_heads, query_heads // key_heads, width).transpose(1, 2, 0, 3)


def body(queries, keys, values, tangent_queries, tangent_keys, tangent_values, doc_start, out_gain):
    rows, query_heads, width = queries.shape
    key_heads = keys.shape[1]
    group = query_heads // key_heads
    scale = width ** (-0.5)
    cycle = lax.axis_size("ctx")
    index = lax.axis_index("ctx")
    block = rows // doc_start.shape[0]
    reach = DOC_DEVS
    features = QH * HD
    query_pos = index * rows + jnp.arange(rows, dtype=jnp.int32)
    own_start = jnp.repeat(doc_start * block, block)
    query_heads_b = heads_first(queries, key_heads)
    slope_heads = heads_first(tangent_queries, key_heads)
    gain_heads = out_gain.reshape(key_heads, group, 1, width)

    def allowed_at(offset):
        key_pos = (index - offset) % cycle * rows + jnp.arange(rows, dtype=jnp.int32)
        return (key_pos[None, :] >= own_start[:, None]) & (key_pos[None, :] <= query_pos[:, None])

    packet = jnp.stack([keys, values, tangent_keys, tangent_values])
    row_zeros = jnp.zeros((key_heads, group, rows), jnp.float32)
    head_zeros = jnp.zeros((key_heads, group, rows, width), jnp.float32)
    state = (
        jnp.full((key_heads, group, rows), -jnp.inf, jnp.float32),
        row_zeros,
        head_zeros,
        head_zeros,
        row_zeros,
    )
    kept = []
    for offset in range(reach + 1):
        if offset > 0:
            packet = passed_along(packet, "ctx", 1)
        kept.append(packet[:2])
        forward_most, forward_total, forward_plain, forward_moving, forward_weighted = state
        forward_key_block = packet[0]
        forward_value_block = packet[1]
        key_slope = packet[2]
        value_slope = packet[3]
        forward_allowed = allowed_at(offset)
        forward_scores = scale * jnp.einsum(
            "kgtd,ukd->kgtu", query_heads_b, forward_key_block, preferred_element_type=jnp.float32
        )
        slopes = scale * (
            jnp.einsum(
                "kgtd,ukd->kgtu", slope_heads, forward_key_block, preferred_element_type=jnp.float32
            )
            + jnp.einsum(
                "kgtd,ukd->kgtu", query_heads_b, key_slope, preferred_element_type=jnp.float32
            )
        )
        new_most = jnp.maximum(
            forward_most, jnp.max(jnp.where(forward_allowed, forward_scores, -jnp.inf), axis=-1)
        )
        decay = jnp.exp(forward_most - new_most)
        weights = jnp.where(forward_allowed, jnp.exp(forward_scores - new_most[..., None]), 0.0)
        forward_total = forward_total * decay + jnp.sum(weights, axis=-1)
        forward_weighted = forward_weighted * decay + jnp.sum(weights * slopes, axis=-1)
        weights_b = weights.astype(jnp.bfloat16)
        mixed_b = (weights * slopes).astype(jnp.bfloat16)
        forward_plain = forward_plain * decay[..., None] + jnp.einsum(
            "kgtu,ukd->kgtd", weights_b, forward_value_block, preferred_element_type=jnp.float32
        )
        forward_moving = (
            forward_moving * decay[..., None]
            + jnp.einsum(
                "kgtu,ukd->kgtd", mixed_b, forward_value_block, preferred_element_type=jnp.float32
            )
            + jnp.einsum(
                "kgtu,ukd->kgtd", weights_b, value_slope, preferred_element_type=jnp.float32
            )
        )
        state = (new_most, forward_total, forward_plain, forward_moving, forward_weighted)
    most, total, plain, moving, weighted = state
    output = plain / total[..., None]
    moved = moving / total[..., None] - (weighted / total)[..., None] * output
    log_norm = most + jnp.log(total)
    own_square = jnp.sum(output * output, axis=(0, 1, 3))
    own_cross = jnp.sum(output * moved, axis=(0, 1, 3))
    square_sum, cross_sum = lax.psum((own_square, own_cross), "head")
    mean_square = square_sum / features + EPSILON
    root = jnp.sqrt(mean_square)[None, None, :, None]
    tangent_y = (
        gain_heads
        * (moved - output * (cross_sum / (features * mean_square))[None, None, :, None])
        / root
    )
    grad_out = gain_heads * tangent_y
    back_sum = lax.psum(jnp.sum(output * grad_out, axis=(0, 1, 3)), "head")
    cotangent = (
        (grad_out - output * (back_sum / (features * mean_square))[None, None, :, None]) / root
    ).astype(jnp.bfloat16)
    row_dot = jnp.sum(cotangent.astype(jnp.float32) * output, axis=-1)
    query_grad = head_zeros
    carried = jnp.stack([keys, values])
    sums = jnp.zeros((2, rows, key_heads, width), jnp.float32)
    for offset in range(reach + 1):
        if offset > 0:
            carried = passed_along(carried, "ctx", 1)
            sums = from_behind(sums.astype(jnp.bfloat16), "ctx", 1).astype(sums.dtype)
        key_block = carried[0]
        allowed = allowed_at(offset)
        scores = scale * jnp.einsum(
            "kgtd,ukd->kgtu", query_heads_b, key_block, preferred_element_type=jnp.float32
        )
        probs = jnp.where(allowed, jnp.exp(scores - log_norm[..., None]), 0.0)
        prob_dot = jnp.einsum(
            "kgtd,ukd->kgtu", cotangent, carried[1], preferred_element_type=jnp.float32
        )
        score_grad = (probs * (prob_dot - row_dot[..., None]) * scale).astype(jnp.bfloat16)
        query_part = jnp.einsum(
            "kgtu,ukd->kgtd", score_grad, key_block, preferred_element_type=jnp.float32
        )
        key_part = jnp.einsum(
            "kgtu,kgtd->ukd", score_grad, query_heads_b, preferred_element_type=jnp.float32
        )
        value_part = jnp.einsum(
            "kgtu,kgtd->ukd",
            probs.astype(jnp.bfloat16),
            cotangent,
            preferred_element_type=jnp.float32,
        )
        query_part, pair_part = (query_part, jnp.stack([key_part, value_part]))
        query_grad = query_grad + query_part
        sums = sums + pair_part
    sums = from_behind(sums.astype(jnp.bfloat16), "ctx", -reach).astype(sums.dtype)
    product_queries = query_grad.transpose(2, 0, 1, 3).reshape(rows, query_heads, width)
    return (product_queries, sums[0], sums[1])


def solution(mesh):
    return jax.shard_map(
        body,
        mesh=mesh,
        in_specs=(
            P("ctx", "head", None),
            P("ctx", "head", None),
            P("ctx", "head", None),
            P("ctx", "head", None),
            P("ctx", "head", None),
            P("ctx", "head", None),
            P("ctx"),
            P("head"),
        ),
        out_specs=(P("ctx", "head", None), P("ctx", "head", None), P("ctx", "head", None)),
        check_vma=False,
    )
```

profile of v0, /device:TPU:36, one launch (start us, length us, event | category | flops | bytes accessed | tf_op | source)
XLA Modules:
  0.0 476.1 jit_solution(13371255747879508345)
XLA Ops:
  3.8 14.9 %collective-permute-start.8 = (bf16[2,256,1,128]{3,1,2,0:T(8,128)(2,1)S(1)}, bf16[2,256,1,128]{3,1,2,0:T(8,128)(2,1)S(1)}, u32[]{:S(2)}, u32[]{:S(2)}) collective-permute-start(bf16[2,256,1,128]{3,1,2,0:T(8,128)(2,1)S(1)} %pad_maximum_fusion.1), channel_id=1, source_target_pairs={{0,8},{8,16},{16,24},{24,32},{32,40},{40,48},{48,56},{56,64},{64,7... | collective-permute-start | bytes 393224 | tf_op jit(solution)/shard_map/ppermute | solution.py:17
  22.3 11.5 %collective-permute-done.8 = bf16[2,256,1,128]{3,1,2,0:T(8,128)(2,1)S(1)} collective-permute-done((bf16[2,256,1,128]{3,1,2,0:T(8,128)(2,1)S(1)}, bf16[2,256,1,128]{3,1,2,0:T(8,128)(2,1)S(1)}, u32[]{:S(2)}, u32[]{:S(2)}) %collective-permute-start.8) | collective-permute-done | bytes 131104 | tf_op jit(solution)/shard_map/ppermute | solution.py:17
  33.8 2.1 collective-permute-start.9
  36.0 13.2 %collective-permute-start.1 = (bf16[4,256,1,128]{3,1,2,0:T(8,128)(2,1)S(1)}, bf16[4,256,1,128]{3,1,2,0:T(8,128)(2,1)S(1)}, u32[]{:S(2)}, u32[]{:S(2)}) collective-permute-start(bf16[4,256,1,128]{3,1,2,0:T(8,128)(2,1)S(1)} %collective-permute-done), channel_id=1, source_target_pairs={{0,8},{8,16},{16,24},{24,32},{32,40},{40,48},{48,56},{56,64},{64,7... | collective-permute-start | bytes 786440 | tf_op jit(solution)/shard_map/ppermute | solution.py:17
  49.5 11.9 %collective-permute-done.9 = bf16[2,256,1,128]{3,1,2,0:T(8,128)(2,1)S(1)} collective-permute-done((bf16[2,256,1,128]{3,1,2,0:T(8,128)(2,1)S(1)}, bf16[2,256,1,128]{3,1,2,0:T(8,128)(2,1)S(1)}, u32[]{:S(2)}, u32[]{:S(2)}) %collective-permute-start.9) | collective-permute-done | bytes 131104 | tf_op jit(solution)/shard_map/ppermute | solution.py:17
  63.6 16.1 %collective-permute-done.10 = bf16[2,256,1,128]{3,1,2,0:T(8,128)(2,1)S(1)} collective-permute-done((bf16[2,256,1,128]{3,1,2,0:T(8,128)(2,1)S(1)}, bf16[2,256,1,128]{3,1,2,0:T(8,128)(2,1)S(1)}, u32[]{:S(2)}, u32[]{:S(2)}) %collective-permute-start.10) | collective-permute-done | bytes 131104 | tf_op jit(solution)/shard_map/ppermute | solution.py:17
  83.9 14.0 %collective-permute-done.11 = bf16[2,256,1,128]{3,1,2,0:T(8,128)(2,1)S(1)} collective-permute-done((bf16[2,256,1,128]{3,1,2,0:T(8,128)(2,1)S(1)}, bf16[2,256,1,128]{3,1,2,0:T(8,128)(2,1)S(1)}, u32[]{:S(2)}, u32[]{:S(2)}) %collective-permute-start.11) | collective-permute-done | bytes 131104 | tf_op jit(solution)/shard_map/ppermute | solution.py:17
  100.1 15.9 %collective-permute-done.12 = bf16[2,256,1,128]{3,1,2,0:T(8,128)(2,1)S(1)} collective-permute-done((bf16[2,256,1,128]{3,1,2,0:T(8,128)(2,1)S(1)}, bf16[2,256,1,128]{3,1,2,0:T(8,128)(2,1)S(1)}, u32[]{:S(2)}, u32[]{:S(2)}) %collective-permute-start.12) | collective-permute-done | bytes 131104 | tf_op jit(solution)/shard_map/ppermute | solution.py:17
  120.2 14.2 %collective-permute-done.13 = bf16[2,256,1,128]{3,1,2,0:T(8,128)(2,1)S(1)} collective-permute-done((bf16[2,256,1,128]{3,1,2,0:T(8,128)(2,1)S(1)}, bf16[2,256,1,128]{3,1,2,0:T(8,128)(2,1)S(1)}, u32[]{:S(2)}, u32[]{:S(2)}) %collective-permute-start.13) | collective-permute-done | bytes 131104 | tf_op jit(solution)/shard_map/ppermute | solution.py:17
  136.6 15.9 %collective-permute-done.14 = bf16[2,256,1,128]{3,1,2,0:T(8,128)(2,1)} collective-permute-done((bf16[2,256,1,128]{3,1,2,0:T(8,128)(2,1)S(1)}, bf16[2,256,1,128]{3,1,2,0:T(8,128)(2,1)}, u32[]{:S(2)}, u32[]{:S(2)}) %collective-permute-start.14) | collective-permute-done | bytes 131104 | tf_op jit(solution)/shard_map/ppermute | solution.py:17
  157.0 19.6 %collective-permute-done.4 = bf16[4,256,1,128]{3,1,2,0:T(8,128)(2,1)S(1)} collective-permute-done((bf16[4,256,1,128]{3,1,2,0:T(8,128)(2,1)S(1)}, bf16[4,256,1,128]{3,1,2,0:T(8,128)(2,1)S(1)}, u32[]{:S(2)}, u32[]{:S(2)}) %collective-permute-start.4) | collective-permute-done | bytes 262176 | tf_op jit(solution)/shard_map/ppermute | solution.py:17
  179.1 17.1 %collective-permute-done.5 = bf16[4,256,1,128]{3,1,2,0:T(8,128)(2,1)S(1)} collective-permute-done((bf16[4,256,1,128]{3,1,2,0:T(8,128)(2,1)S(1)}, bf16[4,256,1,128]{3,1,2,0:T(8,128)(2,1)S(1)}, u32[]{:S(2)}, u32[]{:S(2)}) %collective-permute-start.5) | collective-permute-done | bytes 262176 | tf_op jit(solution)/shard_map/ppermute | solution.py:17
  198.8 17.1 %collective-permute-done.6 = bf16[4,256,1,128]{3,1,2,0:T(8,128)(2,1)S(1)} collective-permute-done((bf16[4,256,1,128]{3,1,2,0:T(8,128)(2,1)S(1)}, bf16[4,256,1,128]{3,1,2,0:T(8,128)(2,1)S(1)}, u32[]{:S(2)}, u32[]{:S(2)}) %collective-permute-start.6) | collective-permute-done | bytes 262176 | tf_op jit(solution)/shard_map/ppermute | solution.py:17
  218.5 16.7 %collective-permute-done.7 = bf16[4,256,1,128]{3,1,2,0:T(8,128)(2,1)S(1)} collective-permute-done((bf16[4,256,1,128]{3,1,2,0:T(8,128)(2,1)S(1)}, bf16[4,256,1,128]{3,1,2,0:T(8,128)(2,1)S(1)}, u32[]{:S(2)}, u32[]{:S(2)}) %collective-permute-start.7) | collective-permute-done | bytes 262176 | tf_op jit(solution)/shard_map/ppermute | solution.py:17
  250.9 31.3 %all-reduce = (f32[256]{0:T(256)S(1)}, f32[256]{0:T(256)S(1)}) all-reduce(f32[256]{0:T(256)S(1)} %get-tuple-element.7, f32[256]{0:T(256)S(1)} %get-tuple-element.6), channel_id=1, replica_groups=mesh['ctx'=64,'head'=8] {'head'}, use_global_device_ids=true, to_apply=%region_30.31 | all-reduce | flops 512 | bytes 4096 | tf_op jit(solution)/shard_map/psum | solution.py:111
  283.1 31.1 %psum.23 = f32[256]{0:T(256)S(1)} all-reduce(f32[256]{0:T(256)S(1)} %multiply_reduce_fusion.1), channel_id=1, replica_groups=mesh['ctx'=64,'head'=8] {'head'}, use_global_device_ids=true, to_apply=%region_32.33 | all-reduce | flops 256 | bytes 2048 | tf_op jit(solution)/shard_map/psum | solution.py:120
  337.9 17.2 %collective-permute-done.17 = bf16[2,256,1,128]{3,1,2,0:T(8,128)(2,1)S(1)} collective-permute-done((bf16[2,256,1,128]{3,1,2,0:T(8,128)(2,1)S(1)}, bf16[2,256,1,128]{3,1,2,0:T(8,128)(2,1)S(1)}, u32[]{:S(2)}, u32[]{:S(2)}) %collective-permute-start.17) | collective-permute-done | bytes 131104 | tf_op jit(solution)/shard_map/ppermute | solution.py:23
  357.4 16.1 %collective-permute-done.18 = bf16[2,256,1,128]{3,1,2,0:T(8,128)(2,1)S(1)} collective-permute-done((bf16[2,256,1,128]{3,1,2,0:T(8,128)(2,1)S(1)}, bf16[2,256,1,128]{3,1,2,0:T(8,128)(2,1)S(1)}, u32[]{:S(2)}, u32[]{:S(2)}) %collective-permute-start.18) | collective-permute-done | bytes 131104 | tf_op jit(solution)/shard_map/ppermute | solution.py:23
  375.7 16.7 %collective-permute-done.19 = bf16[2,256,1,128]{3,1,2,0:T(8,128)(2,1)S(1)} collective-permute-done((bf16[2,256,1,128]{3,1,2,0:T(8,128)(2,1)S(1)}, bf16[2,256,1,128]{3,1,2,0:T(8,128)(2,1)S(1)}, u32[]{:S(2)}, u32[]{:S(2)}) %collective-permute-start.19) | collective-permute-done | bytes 131104 | tf_op jit(solution)/shard_map/ppermute | solution.py:23
  394.7 16.7 %collective-permute-done.20 = bf16[2,256,1,128]{3,1,2,0:T(8,128)(2,1)S(1)} collective-permute-done((bf16[2,256,1,128]{3,1,2,0:T(8,128)(2,1)S(1)}, bf16[2,256,1,128]{3,1,2,0:T(8,128)(2,1)S(1)}, u32[]{:S(2)}, u32[]{:S(2)}) %collective-permute-start.20) | collective-permute-done | bytes 131104 | tf_op jit(solution)/shard_map/ppermute | solution.py:23
  413.6 15.9 %collective-permute-done.21 = bf16[2,256,1,128]{3,1,2,0:T(8,128)(2,1)S(1)} collective-permute-done((bf16[2,256,1,128]{3,1,2,0:T(8,128)(2,1)S(1)}, bf16[2,256,1,128]{3,1,2,0:T(8,128)(2,1)S(1)}, u32[]{:S(2)}, u32[]{:S(2)}) %collective-permute-start.21) | collective-permute-done | bytes 131104 | tf_op jit(solution)/shard_map/ppermute | solution.py:23
  431.8 16.4 %collective-permute-done.22 = bf16[2,256,1,128]{3,1,2,0:T(8,128)(2,1)S(1)} collective-permute-done((bf16[2,256,1,128]{3,1,2,0:T(8,128)(2,1)S(1)}, bf16[2,256,1,128]{3,1,2,0:T(8,128)(2,1)S(1)}, u32[]{:S(2)}, u32[]{:S(2)}) %collective-permute-start.22) | collective-permute-done | bytes 131104 | tf_op jit(solution)/shard_map/ppermute | solution.py:23
  450.5 16.5 %collective-permute-done.23 = bf16[2,256,1,128]{3,1,2,0:T(8,128)(2,1)S(1)} collective-permute-done((bf16[2,256,1,128]{3,1,2,0:T(8,128)(2,1)S(1)}, bf16[2,256,1,128]{3,1,2,0:T(8,128)(2,1)S(1)}, u32[]{:S(2)}, u32[]{:S(2)}) %collective-permute-start.23) | collective-permute-done | bytes 131104 | tf_op jit(solution)/shard_map/ppermute | solution.py:23
  471.3 4.1 collective-permute-done.24
  (200 shorter events, 91.9 us)
Async XLA Ops:
  1.7 34.3 %collective-permute-start = (bf16[4,256,1,128]{3,1,2,0:T(8,128)(2,1)S(1)}, bf16[4,256,1,128]{3,1,2,0:T(8,128)(2,1)S(1)}, u32[]{:S(2)}, u32[]{:S(2)}) collective-permute-start(bf16[4,256,1,128]{3,1,2,0:T(8,128)(2,1)S(1)} %pad_maximum_fusion), channel_id=1, source_target_pairs={{0,8},{8,16},{16,24},{24,32},{32,40},{40,48},{48,56},{56,64},{64,7... | collective-permute-start | bytes 786440 | tf_op jit(solution)/shard_map/ppermute | solution.py:17
  3.8 30.1 %collective-permute-start.8 = (bf16[2,256,1,128]{3,1,2,0:T(8,128)(2,1)S(1)}, bf16[2,256,1,128]{3,1,2,0:T(8,128)(2,1)S(1)}, u32[]{:S(2)}, u32[]{:S(2)}) collective-permute-start(bf16[2,256,1,128]{3,1,2,0:T(8,128)(2,1)S(1)} %pad_maximum_fusion.1), channel_id=1, source_target_pairs={{0,8},{8,16},{16,24},{24,32},{32,40},{40,48},{48,56},{56,64},{64,7... | collective-permute-start | bytes 393224 | tf_op jit(solution)/shard_map/ppermute | solution.py:17
  33.8 27.5 %collective-permute-start.9 = (bf16[2,256,1,128]{3,1,2,0:T(8,128)(2,1)S(1)}, bf16[2,256,1,128]{3,1,2,0:T(8,128)(2,1)S(1)}, u32[]{:S(2)}, u32[]{:S(2)}) collective-permute-start(bf16[2,256,1,128]{3,1,2,0:T(8,128)(2,1)S(1)} %collective-permute-done.8), channel_id=1, source_target_pairs={{0,8},{8,16},{16,24},{24,32},{32,40},{40,48},{48,56},{56,64},{64,7... | collective-permute-start | bytes 393224 | tf_op jit(solution)/shard_map/ppermute | solution.py:17
  36.0 45.6 %collective-permute-start.1 = (bf16[4,256,1,128]{3,1,2,0:T(8,128)(2,1)S(1)}, bf16[4,256,1,128]{3,1,2,0:T(8,128)(2,1)S(1)}, u32[]{:S(2)}, u32[]{:S(2)}) collective-permute-start(bf16[4,256,1,128]{3,1,2,0:T(8,128)(2,1)S(1)} %collective-permute-done), channel_id=1, source_target_pairs={{0,8},{8,16},{16,24},{24,32},{32,40},{40,48},{48,56},{56,64},{64,7... | collective-permute-start | bytes 786440 | tf_op jit(solution)/shard_map/ppermute | solution.py:17
  61.4 18.3 %collective-permute-start.10 = (bf16[2,256,1,128]{3,1,2,0:T(8,128)(2,1)S(1)}, bf16[2,256,1,128]{3,1,2,0:T(8,128)(2,1)S(1)}, u32[]{:S(2)}, u32[]{:S(2)}) collective-permute-start(bf16[2,256,1,128]{3,1,2,0:T(8,128)(2,1)S(1)} %collective-permute-done.9), channel_id=1, source_target_pairs={{0,8},{8,16},{16,24},{24,32},{32,40},{40,48},{48,56},{56,64},{64,7... | collective-permute-start | bytes 393224 | tf_op jit(solution)/shard_map/ppermute | solution.py:17
  79.7 18.2 %collective-permute-start.11 = (bf16[2,256,1,128]{3,1,2,0:T(8,128)(2,1)S(1)}, bf16[2,256,1,128]{3,1,2,0:T(8,128)(2,1)S(1)}, u32[]{:S(2)}, u32[]{:S(2)}) collective-permute-start(bf16[2,256,1,128]{3,1,2,0:T(8,128)(2,1)S(1)} %collective-permute-done.10), channel_id=1, source_target_pairs={{0,8},{8,16},{16,24},{24,32},{32,40},{40,48},{48,56},{56,64},{64,7... | collective-permute-start | bytes 393224 | tf_op jit(solution)/shard_map/ppermute | solution.py:17
  81.6 36.4 %collective-permute-start.2 = (bf16[4,256,1,128]{3,1,2,0:T(8,128)(2,1)S(1)}, bf16[4,256,1,128]{3,1,2,0:T(8,128)(2,1)S(1)}, u32[]{:S(2)}, u32[]{:S(2)}) collective-permute-start(bf16[4,256,1,128]{3,1,2,0:T(8,128)(2,1)S(1)} %collective-permute-done.1), channel_id=1, source_target_pairs={{0,8},{8,16},{16,24},{24,32},{32,40},{40,48},{48,56},{56,64},{64,7... | collective-permute-start | bytes 786440 | tf_op jit(solution)/shard_map/ppermute | solution.py:17
  97.9 18.2 %collective-permute-start.12 = (bf16[2,256,1,128]{3,1,2,0:T(8,128)(2,1)S(1)}, bf16[2,256,1,128]{3,1,2,0:T(8,128)(2,1)S(1)}, u32[]{:S(2)}, u32[]{:S(2)}) collective-permute-start(bf16[2,256,1,128]{3,1,2,0:T(8,128)(2,1)S(1)} %collective-permute-done.11), channel_id=1, source_target_pairs={{0,8},{8,16},{16,24},{24,32},{32,40},{40,48},{48,56},{56,64},{64,7... | collective-permute-start | bytes 393224 | tf_op jit(solution)/shard_map/ppermute | solution.py:17
  116.1 18.3 %collective-permute-start.13 = (bf16[2,256,1,128]{3,1,2,0:T(8,128)(2,1)S(1)}, bf16[2,256,1,128]{3,1,2,0:T(8,128)(2,1)S(1)}, u32[]{:S(2)}, u32[]{:S(2)}) collective-permute-start(bf16[2,256,1,128]{3,1,2,0:T(8,128)(2,1)S(1)} %collective-permute-done.12), channel_id=1, source_target_pairs={{0,8},{8,16},{16,24},{24,32},{32,40},{40,48},{48,56},{56,64},{64,7... | collective-permute-start | bytes 393224 | tf_op jit(solution)/shard_map/ppermute | solution.py:17
  118.0 36.4 %collective-permute-start.3 = (bf16[4,256,1,128]{3,1,2,0:T(8,128)(2,1)S(1)}, bf16[4,256,1,128]{3,1,2,0:T(8,128)(2,1)S(1)}, u32[]{:S(2)}, u32[]{:S(2)}) collective-permute-start(bf16[4,256,1,128]{3,1,2,0:T(8,128)(2,1)S(1)} %collective-permute-done.2), channel_id=1, source_target_pairs={{0,8},{8,16},{16,24},{24,32},{32,40},{40,48},{48,56},{56,64},{64,7... | collective-permute-start | bytes 786440 | tf_op jit(solution)/shard_map/ppermute | solution.py:17
  134.4 18.1 %collective-permute-start.14 = (bf16[2,256,1,128]{3,1,2,0:T(8,128)(2,1)S(1)}, bf16[2,256,1,128]{3,1,2,0:T(8,128)(2,1)}, u32[]{:S(2)}, u32[]{:S(2)}) collective-permute-start(bf16[2,256,1,128]{3,1,2,0:T(8,128)(2,1)S(1)} %collective-permute-done.13), channel_id=1, source_target_pairs={{0,8},{8,16},{16,24},{24,32},{32,40},{40,48},{48,56},{56,64},{64,7... | collective-permute-start | bytes 393224 | tf_op jit(solution)/shard_map/ppermute | solution.py:17
  152.5 173.9 %collective-permute-start.15 = (bf16[2,256,1,128]{3,1,2,0:T(8,128)(2,1)}, bf16[2,256,1,128]{3,1,2,0:T(8,128)(2,1)}, u32[]{:S(2)}, u32[]{:S(2)}) collective-permute-start(bf16[2,256,1,128]{3,1,2,0:T(8,128)(2,1)} %collective-permute-done.14), channel_id=1, source_target_pairs={{0,8},{8,16},{16,24},{24,32},{32,40},{40,48},{48,56},{56,64},{64,7... | collective-permute-start | bytes 393224 | tf_op jit(solution)/shard_map/ppermute | solution.py:17
  154.4 22.2 %collective-permute-start.4 = (bf16[4,256,1,128]{3,1,2,0:T(8,128)(2,1)S(1)}, bf16[4,256,1,128]{3,1,2,0:T(8,128)(2,1)S(1)}, u32[]{:S(2)}, u32[]{:S(2)}) collective-permute-start(bf16[4,256,1,128]{3,1,2,0:T(8,128)(2,1)S(1)} %collective-permute-done.3), channel_id=1, source_target_pairs={{0,8},{8,16},{16,24},{24,32},{32,40},{40,48},{48,56},{56,64},{64,7... | collective-permute-start | bytes 786440 | tf_op jit(solution)/shard_map/ppermute | solution.py:17
  176.6 19.6 %collective-permute-start.5 = (bf16[4,256,1,128]{3,1,2,0:T(8,128)(2,1)S(1)}, bf16[4,256,1,128]{3,1,2,0:T(8,128)(2,1)S(1)}, u32[]{:S(2)}, u32[]{:S(2)}) collective-permute-start(bf16[4,256,1,128]{3,1,2,0:T(8,128)(2,1)S(1)} %collective-permute-done.4), channel_id=1, source_target_pairs={{0,8},{8,16},{16,24},{24,32},{32,40},{40,48},{48,56},{56,64},{64,7... | collective-permute-start | bytes 786440 | tf_op jit(solution)/shard_map/ppermute | solution.py:17
  196.2 19.6 %collective-permute-start.6 = (bf16[4,256,1,128]{3,1,2,0:T(8,128)(2,1)S(1)}, bf16[4,256,1,128]{3,1,2,0:T(8,128)(2,1)S(1)}, u32[]{:S(2)}, u32[]{:S(2)}) collective-permute-start(bf16[4,256,1,128]{3,1,2,0:T(8,128)(2,1)S(1)} %collective-permute-done.5), channel_id=1, source_target_pairs={{0,8},{8,16},{16,24},{24,32},{32,40},{40,48},{48,56},{56,64},{64,7... | collective-permute-start | bytes 786440 | tf_op jit(solution)/shard_map/ppermute | solution.py:17
  215.8 19.4 %collective-permute-start.7 = (bf16[4,256,1,128]{3,1,2,0:T(8,128)(2,1)S(1)}, bf16[4,256,1,128]{3,1,2,0:T(8,128)(2,1)S(1)}, u32[]{:S(2)}, u32[]{:S(2)}) collective-permute-start(bf16[4,256,1,128]{3,1,2,0:T(8,128)(2,1)S(1)} %collective-permute-done.6), channel_id=1, source_target_pairs={{0,8},{8,16},{16,24},{24,32},{32,40},{40,48},{48,56},{56,64},{64,7... | collective-permute-start | bytes 786440 | tf_op jit(solution)/shard_map/ppermute | solution.py:17
  315.9 19.8 %collective-permute-start.16 = (bf16[2,256,1,128]{3,1,2,0:T(8,128)(2,1)S(1)}, bf16[2,256,1,128]{3,1,2,0:T(8,128)(2,1)S(1)}, u32[]{:S(2)}, u32[]{:S(2)}) collective-permute-start(bf16[2,256,1,128]{3,1,2,0:T(8,128)(2,1)S(1)} %pad_maximum_fusion.2), channel_id=1, source_target_pairs={{0,8},{8,16},{16,24},{24,32},{32,40},{40,48},{48,56},{56,64},{64,7... | collective-permute-start | bytes 393224 | tf_op jit(solution)/shard_map/ppermute | solution.py:23
  335.7 19.4 %collective-permute-start.17 = (bf16[2,256,1,128]{3,1,2,0:T(8,128)(2,1)S(1)}, bf16[2,256,1,128]{3,1,2,0:T(8,128)(2,1)S(1)}, u32[]{:S(2)}, u32[]{:S(2)}) collective-permute-start(bf16[2,256,1,128]{3,1,2,0:T(8,128)(2,1)S(1)} %fusion.165), channel_id=1, source_target_pairs={{0,8},{8,16},{16,24},{24,32},{32,40},{40,48},{48,56},{56,64},{64,7... | collective-permute-start | bytes 393224 | tf_op jit(solution)/shard_map/ppermute | solution.py:23
  355.1 18.3 %collective-permute-start.18 = (bf16[2,256,1,128]{3,1,2,0:T(8,128)(2,1)S(1)}, bf16[2,256,1,128]{3,1,2,0:T(8,128)(2,1)S(1)}, u32[]{:S(2)}, u32[]{:S(2)}) collective-permute-start(bf16[2,256,1,128]{3,1,2,0:T(8,128)(2,1)S(1)} %fusion.166), channel_id=1, source_target_pairs={{0,8},{8,16},{16,24},{24,32},{32,40},{40,48},{48,56},{56,64},{64,7... | collective-permute-start | bytes 393224 | tf_op jit(solution)/shard_map/ppermute | solution.py:23
  373.4 19.0 %collective-permute-start.19 = (bf16[2,256,1,128]{3,1,2,0:T(8,128)(2,1)S(1)}, bf16[2,256,1,128]{3,1,2,0:T(8,128)(2,1)S(1)}, u32[]{:S(2)}, u32[]{:S(2)}) collective-permute-start(bf16[2,256,1,128]{3,1,2,0:T(8,128)(2,1)S(1)} %fusion.167), channel_id=1, source_target_pairs={{0,8},{8,16},{16,24},{24,32},{32,40},{40,48},{48,56},{56,64},{64,7... | collective-permute-start | bytes 393224 | tf_op jit(solution)/shard_map/ppermute | solution.py:23
  392.4 19.0 %collective-permute-start.20 = (bf16[2,256,1,128]{3,1,2,0:T(8,128)(2,1)S(1)}, bf16[2,256,1,128]{3,1,2,0:T(8,128)(2,1)S(1)}, u32[]{:S(2)}, u32[]{:S(2)}) collective-permute-start(bf16[2,256,1,128]{3,1,2,0:T(8,128)(2,1)S(1)} %fusion.168), channel_id=1, source_target_pairs={{0,8},{8,16},{16,24},{24,32},{32,40},{40,48},{48,56},{56,64},{64,7... | collective-permute-start | bytes 393224 | tf_op jit(solution)/shard_map/ppermute | solution.py:23
  411.4 18.1 %collective-permute-start.21 = (bf16[2,256,1,128]{3,1,2,0:T(8,128)(2,1)S(1)}, bf16[2,256,1,128]{3,1,2,0:T(8,128)(2,1)S(1)}, u32[]{:S(2)}, u32[]{:S(2)}) collective-permute-start(bf16[2,256,1,128]{3,1,2,0:T(8,128)(2,1)S(1)} %fusion.169), channel_id=1, source_target_pairs={{0,8},{8,16},{16,24},{24,32},{32,40},{40,48},{48,56},{56,64},{64,7... | collective-permute-start | bytes 393224 | tf_op jit(solution)/shard_map/ppermute | solution.py:23
  429.6 18.7 %collective-permute-start.22 = (bf16[2,256,1,128]{3,1,2,0:T(8,128)(2,1)S(1)}, bf16[2,256,1,128]{3,1,2,0:T(8,128)(2,1)S(1)}, u32[]{:S(2)}, u32[]{:S(2)}) collective-permute-start(bf16[2,256,1,128]{3,1,2,0:T(8,128)(2,1)S(1)} %fusion.170), channel_id=1, source_target_pairs={{0,8},{8,16},{16,24},{24,32},{32,40},{40,48},{48,56},{56,64},{64,7... | collective-permute-start | bytes 393224 | tf_op jit(solution)/shard_map/ppermute | solution.py:23
  448.3 18.7 %collective-permute-start.23 = (bf16[2,256,1,128]{3,1,2,0:T(8,128)(2,1)S(1)}, bf16[2,256,1,128]{3,1,2,0:T(8,128)(2,1)S(1)}, u32[]{:S(2)}, u32[]{:S(2)}) collective-permute-start(bf16[2,256,1,128]{3,1,2,0:T(8,128)(2,1)S(1)} %fusion.171), channel_id=1, source_target_pairs={{0,8},{8,16},{16,24},{24,32},{32,40},{40,48},{48,56},{56,64},{64,7... | collective-permute-start | bytes 393224 | tf_op jit(solution)/shard_map/ppermute | solution.py:23
  (19 other events, 56.2 us)
where the time goes:
time: 478 us; the launch traced here: 476 us
  waiting for transfers between devices  290 us (61%)
  starting transfers between devices  72.7 us (15%)
  blocking collectives  62.4 us (13%)
  matrix products  37.4 us (8%)
  local copies, waits for them, and re-layouts  7.6 us (2%)
    ppermute x16, waiting for transfers between devices, passed_along(): lax.ppermute(value, axis, [(source, source + steps) for source in range(l...  170 us
    ppermute x9, waiting for transfers between devices, from_behind(): return lax.ppermute(value, axis, pairs)  120 us
    ppermute x16, starting transfers between devices, passed_along(): lax.ppermute(value, axis, [(source, source + steps) for source in range(l...  55.4 us
    psum x1, blocking collectives, body(): square_sum, cross_sum = lax.psum((own_square, own_cross), 'head')  31.3 us
    psum x1, blocking collectives, body(): back_sum = lax.psum(jnp.sum(output * grad_out, axis=(0, 1, 3)), 'head')  31.1 us
    ppermute x9, starting transfers between devices, from_behind(): return lax.ppermute(value, axis, pairs)  17.3 us
  transfers between devices with their start and end apart: 25, of which 19 were waited for; matrix products, arithmetic and copies ran while one was open for 9% of the time, Pallas kernels for 0%

commit v1 on v0

v1 whole, which is shorter than its diff:
```python
import functools

import jax
import jax.numpy as jnp
from jax import lax
from jax.experimental import pallas as pl
from jax.experimental.pallas import tpu as pltpu
from jax.sharding import PartitionSpec as P

MESH = pl.DeviceIdType.MESH
FEATURES = 4096
EPSILON = 1e-06
LOG2E = 1.4426950408889634
MASKED = -1e30
ROWS = 1024
TILE = 256
TOK = 256
HD = 128

F32 = jnp.float32
BF16 = jnp.bfloat16

PHASES = (
    ((0, 0, 256),),
    ((1, 0, 256), (2, 0, 256)),
    ((3, 128, 128), (4, 0, 256)),
    ((5, 0, 128), (6, 0, 128)),
    ((7, 0, 128), (8, 0, 128)),
    ((5, 128, 128), (6, 128, 128)),
    ((7, 128, 128), (8, 128, 128)),
)
LAST = len(PHASES) - 1
CHUNKS = 4


def joined(pieces):
    return pieces[0] if len(pieces) == 1 else jnp.concatenate(pieces, axis=0)


def dot_nt(a, b):
    return lax.dot_general(a, b, (((1,), (1,)), ((), ())), preferred_element_type=F32)


def dot_tn(a, b):
    return lax.dot_general(a, b, (((0,), (0,)), ((), ())), preferred_element_type=F32)


def dot(a, b):
    return lax.dot_general(a, b, (((1,), (0,)), ((), ())), preferred_element_type=F32)


def split(x):
    hi = x.astype(BF16)
    return hi, (x - hi.astype(F32)).astype(BF16)


def kernel(
    contexts, heads,
    q_in, k_in, v_in, tq_in, tk_in, tv_in, doc_in, gain_in,
    dq_out, dk_out, dv_out,
    doc_ref, gain_ref, blocks, tqq, kept, most, acc, norms, grads, gains, pick, stat_out, stat_in,
    scaled, slope, parts, back_out, back_in,
    load_sem, fwd_send, fwd_recv, stat_send, stat_recv, back_send, back_recv,
):
    c = lax.axis_index("ctx")
    h = lax.axis_index("head")
    core = lax.rem(c, 2)
    scale = HD ** (-0.5)

    def ctx(shift):
        return (lax.rem(c + contexts + shift, contexts), h)

    partner = (c + 1 - 2 * core, h)
    mates = [(c, lax.rem(h + i, heads)) for i in range(1, heads)]
    barrier = pltpu.get_barrier_semaphore()
    peers = [ctx(2), ctx(-2), ctx(4), ctx(-4), partner] + mates
    for peer in peers:
        pl.semaphore_signal(barrier, inc=1, device_id=peer, device_id_type=MESH)

    loads = []
    places = (
        (k_in, blocks.at[0, :, 0:128]), (tk_in, blocks.at[0, :, 128:256]),
        (v_in, blocks.at[0, :, 256:384]), (tv_in, blocks.at[0, :, 384:512]),
        (tq_in, tqq.at[:, 0:128]), (q_in, tqq.at[:, 128:256]), (doc_in, doc_ref), (gain_in, gain_ref),
    )
    for i, (src, dst) in enumerate(places):
        load = pltpu.make_async_copy(src, dst, load_sem.at[i])
        load.start()
        loads.append(load)

    def remote(src, dst, send, recv, peer):
        return pltpu.make_async_remote_copy(
            src_ref=src, dst_ref=dst, send_sem=send, recv_sem=recv, device_id=peer, device_id_type=MESH
        )

    count = iter(range(100))

    def fwd(src, dst, peer, chunks):
        copies = []
        for j in range(chunks):
            rows = pl.ds(j * (TOK // chunks), TOK // chunks)
            i = next(count)
            copies.append(remote(
                blocks.at[src, rows], blocks.at[dst, rows], fwd_send.at[i], fwd_recv.at[i], peer
            ))
        return copies

    cross = fwd(0, 5, ctx(2), CHUNKS)
    hop6 = fwd(5, 7, ctx(4), CHUNKS)
    side2 = fwd(5, 6, partner, CHUNKS)
    side6 = fwd(7, 8, partner, CHUNKS)
    (hop4,), (hop8,) = fwd(0, 1, ctx(4), 1), fwd(1, 3, ctx(4), 1)
    (side4,), (side8,) = fwd(1, 2, partner, 1), fwd(3 * core, 4, partner, 1)

    offsets = (0, 4, 3 + 2 * core, 8, 7 - 6 * core, 2, 1 + 2 * core, 6, 5 + 2 * core)

    for load in loads[:4]:
        load.wait()
    pl.semaphore_wait(barrier, len(peers))
    for copy in cross:
        copy.start()
    hop4.start()
    for load in loads[4:]:
        load.wait()

    gain = gain_ref[...]
    four = jnp.concatenate([gain[:, 128 * i : 128 * i + 128] for i in range(4)], axis=0)
    eight = jnp.concatenate([four, four], axis=0)
    eight = eight * eight
    for i in range(512 // 8):
        gains[pl.ds(i * 8, 8), :] = eight
    row_token = lax.broadcasted_iota(jnp.int32, (512, 128), 0) // 4
    lane = lax.broadcasted_iota(jnp.int32, (512, 128), 1)
    pick[...] = jnp.where(row_token == lane, 1.0, 0.0).astype(BF16)
    parts[3, 0:128, :] = jnp.zeros((128, 256), F32)

    def forward(phase, low=0, high=ROWS // TILE):
        pieces_of = PHASES[phase]

        def step(i, carry):
            rows = pl.ds(pl.multiple_of(i * TILE, TILE), TILE)
            first = doc_ref[i // 2]
            both = tqq[rows, :]
            keys = joined([blocks[s, r : r + n, 0:256] for s, r, n in pieces_of])
            vals = joined([blocks[s, r : r + n, 256:512] for s, r, n in pieces_of])
            scores = dot_nt(both[:, 128:256], keys[:, 0:128]) * (scale * LOG2E)
            slopes = dot_nt(both, keys)
            pieces = []
            for s, r, n in pieces_of:
                for block in range(r // 128, (r + n) // 128):
                    j = len(pieces)
                    kb = 2 * (c - offsets[s]) + block
                    piece = scores[:, 128 * j : 128 * j + 128]
                    piece = piece + jnp.where(kb >= first, 0.0, MASKED).astype(F32)
                    if phase == 0:
                        token = i * (TILE // 4) + lax.broadcasted_iota(jnp.int32, (TILE, 128), 0) // 4
                        key = 128 * block + lax.broadcasted_iota(jnp.int32, (TILE, 128), 1)
                        piece = jnp.where(key <= token, piece, MASKED)
                    pieces.append(piece)
            top = pieces[0]
            for piece in pieces[1:]:
                top = jnp.maximum(top, piece)
            new = jnp.max(top, axis=1, keepdims=True)
            if phase > 0:
                old = most[phase - 1, rows, :][:, 0:1]
                new = jnp.maximum(old, new)
                decay = jnp.exp2(old - new)
            most[phase, rows, :] = jnp.broadcast_to(new, (TILE, 128))
            total = jnp.zeros((TILE, 128), F32)
            weighted = jnp.zeros((TILE, 128), F32)
            plain, mixed = [], []
            for j, piece in enumerate(pieces):
                weight = jnp.exp2(piece - new)
                mix = weight * slopes[:, 128 * j : 128 * j + 128]
                total = total + weight
                weighted = weighted + mix
                plain.append(weight.astype(BF16))
                mixed.append(mix.astype(BF16))
            plain = jnp.concatenate(plain, axis=1)
            mixed = jnp.concatenate(mixed, axis=1)
            at = 0
            for s, r, n in pieces_of:
                kept[rows, s * TOK + r : s * TOK + r + n] = plain[:, at : at + n]
                at += n
            product = dot(plain, vals)
            moving = product[:, 128:256] + scale * dot(mixed, vals[:, 0:128])
            stable = product[:, 0:128]
            if phase > 0:
                stable = stable + acc[rows, 0:128] * decay
                moving = moving + acc[rows, 128:256] * decay
                total = total + norms[rows, 0:128] * decay
                weighted = weighted + norms[rows, 128:256] * decay
            acc[rows, 0:128] = stable
            acc[rows, 128:256] = moving
            norms[rows, 0:128] = total
            norms[rows, 128:256] = weighted
            return carry

        lax.fori_loop(low, high, step, 0)

    def stat_copy(half, i):
        return remote(
            stat_out.at[half], stat_in.at[half, h],
            stat_send.at[half * heads + i], stat_recv.at[half * heads + h], mates[i - 1],
        )

    def stat_arrival(half, source):
        return remote(
            stat_out.at[half], stat_in.at[half, source],
            stat_send.at[half * heads], stat_recv.at[half * heads + source], mates[0],
        )

    def finish(half):
        rows = pl.ds(half * 512, 512)
        inverse = 1.0 / jnp.sum(norms[rows, 0:128], axis=1, keepdims=True)
        center = jnp.sum(norms[rows, 128:256], axis=1, keepdims=True) * scale
        output = acc[rows, 0:128] * inverse
        moved = acc[rows, 128:256] * inverse - (center * inverse) * output
        acc[rows, 0:128] = output
        acc[rows, 128:256] = moved
        norms[rows, 0:128] = jnp.broadcast_to(inverse, (512, 128))
        squared = gains[...]
        square = output * output
        cross_term = output * moved
        terms = [split(x) for x in (square, cross_term, squared * cross_term, squared * square)]
        right = jnp.concatenate([t[0] for t in terms] + [t[1] for t in terms], axis=1)
        line = lax.broadcasted_iota(jnp.int32, (8, 1024), 0)
        place = lax.broadcasted_iota(jnp.int32, (8, 1024), 1) // 128
        left = jnp.where(lax.rem(place, 4) == line, 1.0, 0.0).astype(BF16)
        per_row = dot_nt(left, right)
        hi, lo = split(per_row)
        stat_out[half] = dot(hi, pick[...]) + dot(lo, pick[...])
        for i in range(1, heads):
            stat_copy(half, i).start()

    def cotangent(half):
        rows = pl.ds(half * 512, 512)
        sums = stat_out[half]
        for i in range(1, heads):
            source = lax.rem(h + i, heads)
            stat_arrival(half, source).wait_recv()
            sums = sums + stat_in[half, source]
        inverse_square = 1.0 / (sums[0:1] / FEATURES + EPSILON)
        along = inverse_square * sums[1:2] / FEATURES
        back = inverse_square * inverse_square * (sums[2:3] - along * sums[3:4]) / FEATURES
        sides = []
        for value in (inverse_square, along, back):
            wide = jnp.broadcast_to(value, (128, 128))
            hi, lo = split(wide)
            sides.append(jnp.concatenate([hi, lo], axis=1))
        both = jnp.concatenate([pick[...], pick[...]], axis=1)
        spread = dot_nt(both, jnp.concatenate(sides, axis=0))
        output = acc[rows, 0:128]
        moved = acc[rows, 128:256]
        grads[rows, :] = (
            spread[:, 0:128] * (gains[...] * (moved - spread[:, 128:256] * output))
            - spread[:, 256:384] * output
        )

    forward(0)
    hop4.wait_recv()
    hop8.start()
    side4.start()
    side4.wait_recv()
    forward(1)
    hop8.wait_recv()
    side8.start()
    side8.wait_recv()
    forward(2)
    for part in range(2):
        span = range(part * CHUNKS // 2, (part + 1) * CHUNKS // 2)
        for j in span:
            cross[j].wait_recv()
            hop6[j].start()
            side2[j].start()
        for j in span:
            side2[j].wait_recv()
        forward(3 + 2 * part)
        for j in span:
            hop6[j].wait_recv()
            side6[j].start()
        for j in span:
            side6[j].wait_recv()
        if part == 0:
            forward(4)
    forward(LAST, 0, 2)
    finish(0)
    forward(LAST, 2, 4)
    finish(1)

    def backward_rows(phase, first, low=0, high=ROWS // TILE):
        pieces_of = PHASES[phase]
        width = sum(n for s, r, n in pieces_of)
        spot = phase // 2 % 2

        def step(i, carry):
            rows = pl.ds(pl.multiple_of(i * TILE, TILE), TILE)
            keys = joined([blocks[s, r : r + n, 0:128] for s, r, n in pieces_of])
            vals = joined([blocks[s, r : r + n, 256:384] for s, r, n in pieces_of])
            factor = norms[rows, 0:1]
            if phase < LAST:
                factor = factor * jnp.exp2(most[phase, rows, :][:, 0:1] - most[LAST, rows, :][:, 0:1])
            part = (factor * grads[rows, :]).astype(BF16)
            scaled[spot, rows, :] = part
            row_dot = jnp.sum(part.astype(F32) * acc[rows, 0:128], axis=1, keepdims=True)
            weight = jnp.concatenate([kept[rows, s * TOK + r : s * TOK + r + n] for s, r, n in pieces_of], axis=1)
            grad = (weight.astype(F32) * (dot_nt(part, vals) - row_dot)).astype(BF16)
            slope[spot, rows, 0:width] = grad
            product = dot(grad, keys) * scale
            if first:
                dq_out[rows, :] = product
            else:
                dq_out[rows, :] = dq_out[rows, :] + product
            return carry

        lax.fori_loop(low, high, step, 0)

    def backward_keys(phase):
        spot = phase // 2 % 2
        at = 0
        for s, r, n in PHASES[phase]:
            parts[s, r : r + n, 0:128] = dot_tn(slope[spot, :, at : at + n], tqq[:, 128:256]) * scale
            parts[s, r : r + n, 128:256] = dot_tn(kept[:, s * TOK + r : s * TOK + r + n], scaled[spot])
            at += n

    def backward(phase):
        backward_rows(phase, False)
        backward_keys(phase)

    tags = iter(range(100))

    def back(i, peer, chunks=1):
        copies = []
        for j in range(chunks):
            rows = pl.ds(j * (TOK // chunks), TOK // chunks)
            tag = next(tags)
            copy = remote(
                back_out.at[i, rows], back_in.at[i, rows], back_send.at[tag], back_recv.at[tag], peer
            )
            copies.append((copy, i, slice(j * (TOK // chunks), (j + 1) * (TOK // chunks))))
        return copies

    side_back = [back(0, partner), back(1, partner), back(2, partner, 2), back(3, partner, 2)]
    home6, home8, home4 = back(4, ctx(-4), 2), back(5, ctx(-4)), back(6, ctx(-4))
    home2 = back(7, ctx(-2), 2)

    def send(item, value):
        copy, i, rows = item
        back_out[i, rows, :] = value.astype(BF16)
        copy.start()

    def got(item):
        copy, i, rows = item
        copy.wait_recv()
        return back_in[i, rows, :].astype(F32)

    on_one = jnp.where(core == 1, 1.0, 0.0).astype(F32)
    half = (slice(0, 128), slice(128, 256))
    cotangent(0)
    backward_rows(4, True, 0, 2)
    backward_rows(6, False, 0, 2)
    cotangent(1)
    backward_rows(4, True, 2, 4)
    backward_keys(4)
    send(side_back[3][0], parts[8, half[0], :])
    backward_rows(6, False, 2, 4)
    backward_keys(6)
    send(side_back[3][1], parts[8, half[1], :])
    send(home6[0], parts[7, half[0], :] + got(side_back[3][0]))
    backward(3)
    send(side_back[2][0], parts[6, half[0], :])
    send(home6[1], parts[7, half[1], :] + got(side_back[3][1]))
    backward(5)
    send(side_back[2][1], parts[6, half[1], :])
    for j in range(2):
        send(home2[j], parts[5, half[j], :] + got(side_back[2][j]) + got(home6[j]))
    backward(2)
    send(side_back[1][0], parts[4])
    shared = got(side_back[1][0])
    send(home8[0], parts[3] + on_one * shared)
    backward(1)
    send(side_back[0][0], parts[2])
    send(home4[0], parts[1] + got(side_back[0][0]) + got(home8[0]))
    backward(0)
    own = parts[0] + (1.0 - on_one) * back_in[1].astype(F32) + got(home4[0])
    for j in range(2):
        total = own[half[j], :] + got(home2[j])
        dk_out[half[j], :] = total[:, 0:128]
        dv_out[half[j], :] = total[:, 128:256]

    for copy in cross + [hop4, hop8] + hop6 + [side4, side8] + side2 + side6:
        copy.wait_send()
    for part in range(2):
        for i in range(1, heads):
            stat_copy(part, i).wait_send()
    for group in side_back + [home6, home8, home4, home2]:
        for copy, _, _ in group:
            copy.wait_send()


def hand_on(*refs):
    ins, outs, held, sems = refs[0:3], refs[3:6], refs[6:9], refs[9]
    copies = []
    for i in range(3):
        copies.append((
            pltpu.make_async_copy(ins[i], held[i], sems.at[0, i]),
            pltpu.make_async_copy(held[i], outs[i], sems.at[1, i]),
        ))
    for into, _ in copies:
        into.start()
    for into, out in copies:
        into.wait()
        out.start()
    for _, out in copies:
        out.wait()


def solution(mesh):
    contexts, heads = mesh.shape["ctx"], mesh.shape["head"]

    def body(queries, keys, values, tangent_queries, tangent_keys, tangent_values, doc_start, out_gain):
        any_space = pl.BlockSpec(memory_space=pl.ANY)
        vmem = pl.BlockSpec(memory_space=pltpu.VMEM)
        sems = pltpu.SemaphoreType.DMA
        dq, dk, dv = pl.pallas_call(
            functools.partial(kernel, contexts, heads),
            name="gauss_newton",
            out_shape=(
                jax.ShapeDtypeStruct((ROWS, HD), F32),
                jax.ShapeDtypeStruct((TOK, HD), F32),
                jax.ShapeDtypeStruct((TOK, HD), F32),
            ),
            in_specs=[any_space] * 8,
            out_specs=(vmem, vmem, vmem),
            scratch_shapes=[
                pltpu.SMEM((2,), jnp.int32),
                pltpu.VMEM((1, 512), F32),
                pltpu.VMEM((9, TOK, 512), BF16),
                pltpu.VMEM((ROWS, 256), BF16),
                pltpu.VMEM((ROWS, 9 * TOK), BF16),
                pltpu.VMEM((len(PHASES), ROWS, 128), F32),
                pltpu.VMEM((ROWS, 256), F32),
                pltpu.VMEM((ROWS, 256), F32),
                pltpu.VMEM((ROWS, 128), F32),
                pltpu.VMEM((512, 128), F32),
                pltpu.VMEM((512, 128), BF16),
                pltpu.VMEM((2, 8, 128), F32),
                pltpu.VMEM((2, heads, 8, 128), F32),
                pltpu.VMEM((2, ROWS, 128), BF16),
                pltpu.VMEM((2, ROWS, 512), BF16),
                pltpu.VMEM((9, TOK, 256), F32),
                pltpu.VMEM((8, TOK, 256), BF16),
                pltpu.VMEM((8, TOK, 256), BF16),
                sems((8,)), sems((4 * CHUNKS + 4,)), sems((4 * CHUNKS + 4,)),
                sems((2 * heads,)), sems((2 * heads,)), sems((12,)), sems((12,)),
            ],
            compiler_params=pltpu.CompilerParams(
                collective_id=0, has_side_effects=True, vmem_limit_bytes=60 * 1024 * 1024
            ),
        )(
            queries.reshape(ROWS, HD), keys.reshape(TOK, HD), values.reshape(TOK, HD),
            tangent_queries.reshape(ROWS, HD), tangent_keys.reshape(TOK, HD),
            tangent_values.reshape(TOK, HD), doc_start, out_gain.reshape(1, 512),
        )
        dq, dk, dv = pl.pallas_call(
            hand_on,
            name="hand_on",
            out_shape=tuple(jax.ShapeDtypeStruct(x.shape, F32) for x in (dq, dk, dv)),
            in_specs=[any_space] * 3,
            out_specs=(any_space,) * 3,
            scratch_shapes=[pltpu.VMEM(x.shape, F32) for x in (dq, dk, dv)] + [sems((2, 3))],
        )(dq, dk, dv)
        return dq.reshape(TOK, 4, HD), dk.reshape(TOK, 1, HD), dv.reshape(TOK, 1, HD)

    wide = P("ctx", "head", None)
    return jax.shard_map(
        body,
        mesh=mesh,
        in_specs=(wide, wide, wide, wide, wide, wide, P("ctx"), P("head")),
        out_specs=(wide, wide, wide),
        check_vma=False,
    )
```

time: 478 us -> 93.9 us (0.20)
  the two profiles are of different devices: /device:TPU:36 before, /device:TPU:9 now
where the time goes in v1:
time: 93.9 us; the launch traced here: 93.8 us
  Pallas kernels  93.1 us (99%)
    pallas_call x1, Pallas kernels, body(): pl.pallas_call(functools.partial(kernel, contexts, heads), name='gauss_ne...  91.1 us
    pallas_call x1, Pallas kernels, body(): pl.pallas_call(hand_on, name='hand_on', out_shape=tuple((jax.ShapeDtypeSt...  1.96 us

profile of v1, /device:TPU:9, one launch (start us, length us, event | category | flops | bytes accessed | tf_op | source)
XLA Modules:
  0.0 93.8 jit_solution(9818510311822989367)
XLA Ops:
  0.6 91.1 %gauss_newton.1 = (f32[1024,128]{1,0:T(8,128)}, f32[256,128]{1,0:T(8,128)}, f32[256,128]{1,0:T(8,128)}) custom-call(bf16[1024,128]{1,0:T(8,128)(2,1)} %bitcast.14, bf16[256,128]{1,0:T(8,128)(2,1)} %bitcast.16, bf16[256,128]{1,0:T(8,128)(2,1)} %bitcast.17, bf16[1024,128]{1,0:T(8,128)(2,1)} %bitcast.15, bf16[256,128]{1,0:T(8,128)(2,1)} %bitcast.18, ...), custom_call_target="tpu_custom_call" | custom-call | tf_op jit(solution)/shard_map/gauss_newton/pallas_call | solution.py:425
  91.8 2.0 %hand_on.1 = (f32[1024,128]{1,0:T(8,128)}, f32[256,128]{1,0:T(8,128)}, f32[256,128]{1,0:T(8,128)}) custom-call(f32[1024,128]{1,0:T(8,128)} %get-tuple-element.9.refs_0_, f32[256,128]{1,0:T(8,128)} %get-tuple-element.10.refs_1_, f32[256,128]{1,0:T(8,128)} %get-tuple-element.11.refs_2_), custom_call_target="tpu_custom_call" | custom-call | tf_op jit(solution)/shard_map/hand_on/pallas_call | solution.py:465

commit v2 on v1

--- a/solution.py
+++ b/solution.py
@@ -13,7 +13,7 @@
 LOG2E = 1.4426950408889634
 MASKED = -1e30
 ROWS = 1024
-TILE = 256
+TILE = 512
 TOK = 256
 HD = 128
 
@@ -24,13 +24,12 @@
     ((0, 0, 256),),
     ((1, 0, 256), (2, 0, 256)),
     ((3, 128, 128), (4, 0, 256)),
-    ((5, 0, 128), (6, 0, 128)),
-    ((7, 0, 128), (8, 0, 128)),
-    ((5, 128, 128), (6, 128, 128)),
-    ((7, 128, 128), (8, 128, 128)),
+    ((5, 0, 256), (6, 0, 256)),
+    ((7, 0, 256), (8, 0, 256)),
 )
 LAST = len(PHASES) - 1
-CHUNKS = 4
+CHUNKS = 8
+BACK = 4
 
 
 def joined(pieces):
@@ -60,7 +59,7 @@
     dq_out, dk_out, dv_out,
     doc_ref, gain_ref, blocks, tqq, kept, most, acc, norms, grads, gains, pick, stat_out, stat_in,
     scaled, slope, parts, back_out, back_in,
-    load_sem, fwd_send, fwd_recv, stat_send, stat_recv, back_send, back_recv,
+    dq_held, load_sem, fwd_send, fwd_recv, stat_send, stat_recv, back_send, back_recv,
 ):
     c = lax.axis_index("ctx")
     h = lax.axis_index("head")
@@ -139,7 +138,7 @@
 
         def step(i, carry):
             rows = pl.ds(pl.multiple_of(i * TILE, TILE), TILE)
-            first = doc_ref[i // 2]
+            first = doc_ref[i * TILE // 512]
             both = tqq[rows, :]
             keys = joined([blocks[s, r : r + n, 0:256] for s, r, n in pieces_of])
             vals = joined([blocks[s, r : r + n, 256:512] for s, r, n in pieces_of])
@@ -265,33 +264,34 @@
     forward(1)
     hop8.wait_recv()
     side8.start()
-    side8.wait_recv()
-    forward(2)
     for part in range(2):
-        span = range(part * CHUNKS // 2, (part + 1) * CHUNKS // 2)
-        for j in span:
+        for j in range(part * CHUNKS // 2, (part + 1) * CHUNKS // 2):
             cross[j].wait_recv()
             hop6[j].start()
             side2[j].start()
-        for j in span:
-            side2[j].wait_recv()
-        forward(3 + 2 * part)
-        for j in span:
-            hop6[j].wait_recv()
-            side6[j].start()
-        for j in span:
-            side6[j].wait_recv()
         if part == 0:
-            forward(4)
-    forward(LAST, 0, 2)
+            side8.wait_recv()
+            forward(2)
+    for j in range(CHUNKS // 2):
+        hop6[j].wait_recv()
+        side6[j].start()
+    for j in range(CHUNKS):
+        side2[j].wait_recv()
+    forward(3)
+    for j in range(CHUNKS // 2, CHUNKS):
+        hop6[j].wait_recv()
+        side6[j].start()
+    for j in range(CHUNKS):
+        side6[j].wait_recv()
+    middle = 512 // TILE
+    forward(LAST, 0, middle)
     finish(0)
-    forward(LAST, 2, 4)
+    forward(LAST, middle, 2 * middle)
     finish(1)
 
     def backward_rows(phase, first, low=0, high=ROWS // TILE):
         pieces_of = PHASES[phase]
         width = sum(n for s, r, n in pieces_of)
-        spot = phase // 2 % 2
 
         def step(i, carry):
             rows = pl.ds(pl.multiple_of(i * TILE, TILE), TILE)
@@ -301,31 +301,25 @@
             if phase < LAST:
                 factor = factor * jnp.exp2(most[phase, rows, :][:, 0:1] - most[LAST, rows, :][:, 0:1])
             part = (factor * grads[rows, :]).astype(BF16)
-            scaled[spot, rows, :] = part
+            scaled[rows, :] = part
             row_dot = jnp.sum(part.astype(F32) * acc[rows, 0:128], axis=1, keepdims=True)
             weight = jnp.concatenate([kept[rows, s * TOK + r : s * TOK + r + n] for s, r, n in pieces_of], axis=1)
             grad = (weight.astype(F32) * (dot_nt(part, vals) - row_dot)).astype(BF16)
-            slope[spot, rows, 0:width] = grad
+            slope[rows, 0:width] = grad
             product = dot(grad, keys) * scale
             if first:
-                dq_out[rows, :] = product
+                dq_held[rows, :] = product
             else:
-                dq_out[rows, :] = dq_out[rows, :] + product
+                dq_held[rows, :] = dq_held[rows, :] + product
             return carry
 
         lax.fori_loop(low, high, step, 0)
 
-    def backward_keys(phase):
-        spot = phase // 2 % 2
-        at = 0
-        for s, r, n in PHASES[phase]:
-            parts[s, r : r + n, 0:128] = dot_tn(slope[spot, :, at : at + n], tqq[:, 128:256]) * scale
-            parts[s, r : r + n, 128:256] = dot_tn(kept[:, s * TOK + r : s * TOK + r + n], scaled[spot])
-            at += n
-
-    def backward(phase):
-        backward_rows(phase, False)
-        backward_keys(phase)
+    def backward_keys(phase, which):
+        at = sum(n for _, _, n in PHASES[phase][:which])
+        s, r, n = PHASES[phase][which]
+        parts[s, r : r + n, 0:128] = dot_tn(slope[:, at : at + n], tqq[:, 128:256]) * scale
+        parts[s, r : r + n, 128:256] = dot_tn(kept[:, s * TOK + r : s * TOK + r + n], scaled[...])
 
     tags = iter(range(100))
 
@@ -341,58 +335,77 @@
         return copies
 
     side_back = [back(0, partner), back(1, partner), back(2, partner, 2), back(3, partner, 2)]
-    home6, home8, home4 = back(4, ctx(-4), 2), back(5, ctx(-4)), back(6, ctx(-4))
-    home2 = back(7, ctx(-2), 2)
+    home6, home8, home4 = back(4, ctx(-4), BACK), back(5, ctx(-4)), back(6, ctx(-4))
+    home2 = back(7, ctx(-2), BACK)
 
     def send(item, value):
         copy, i, rows = item
         back_out[i, rows, :] = value.astype(BF16)
         copy.start()
 
+    def send_all(items, value):
+        for item in items:
+            send(item, value[item[2], :])
+
+    def got_all(items):
+        return joined([got(item) for item in items])
+
     def got(item):
         copy, i, rows = item
         copy.wait_recv()
         return back_in[i, rows, :].astype(F32)
 
     on_one = jnp.where(core == 1, 1.0, 0.0).astype(F32)
-    half = (slice(0, 128), slice(128, 256))
+    quarter = [item[2] for item in home2]
     cotangent(0)
-    backward_rows(4, True, 0, 2)
-    backward_rows(6, False, 0, 2)
+    backward_rows(4, True, 0, middle)
     cotangent(1)
-    backward_rows(4, True, 2, 4)
-    backward_keys(4)
-    send(side_back[3][0], parts[8, half[0], :])
-    backward_rows(6, False, 2, 4)
-    backward_keys(6)
-    send(side_back[3][1], parts[8, half[1], :])
-    send(home6[0], parts[7, half[0], :] + got(side_back[3][0]))
-    backward(3)
-    send(side_back[2][0], parts[6, half[0], :])
-    send(home6[1], parts[7, half[1], :] + got(side_back[3][1]))
-    backward(5)
-    send(side_back[2][1], parts[6, half[1], :])
+    backward_rows(4, True, middle, 2 * middle)
+    backward_keys(4, 1)
+    send_all(side_back[3], parts[8])
+    backward_keys(4, 0)
     for j in range(2):
-        send(home2[j], parts[5, half[j], :] + got(side_back[2][j]) + got(home6[j]))
-    backward(2)
-    send(side_back[1][0], parts[4])
-    shared = got(side_back[1][0])
-    send(home8[0], parts[3] + on_one * shared)
-    backward(1)
-    send(side_back[0][0], parts[2])
-    send(home4[0], parts[1] + got(side_back[0][0]) + got(home8[0]))
-    backward(0)
-    own = parts[0] + (1.0 - on_one) * back_in[1].astype(F32) + got(home4[0])
+        shared = got(side_back[3][j])
+        for k in range(j * BACK // 2, (j + 1) * BACK // 2):
+            at = quarter[k].start - j * 128
+            send(home6[k], parts[7, quarter[k], :] + shared[at : at + TOK // BACK, :])
+    backward_rows(3, False)
+    backward_keys(3, 1)
+    send_all(side_back[2], parts[6])
+    backward_keys(3, 0)
     for j in range(2):
-        total = own[half[j], :] + got(home2[j])
-        dk_out[half[j], :] = total[:, 0:128]
-        dv_out[half[j], :] = total[:, 128:256]
+        shared = got(side_back[2][j])
+        for k in range(j * BACK // 2, (j + 1) * BACK // 2):
+            at = quarter[k].start - j * 128
+            value = parts[5, quarter[k], :] + shared[at : at + TOK // BACK, :]
+            send(home2[k], value + got(home6[k]))
+    backward_rows(2, False)
+    backward_keys(2, 1)
+    send_all(side_back[1], parts[4])
+    backward_keys(2, 0)
+    send_all(home8, parts[3] + on_one * got_all(side_back[1]))
+    backward_rows(1, False)
+    backward_keys(1, 1)
+    send_all(side_back[0], parts[2])
+    backward_keys(1, 0)
+    send_all(home4, parts[1] + got_all(side_back[0]) + got_all(home8))
+    backward_rows(0, False)
+    leave = pltpu.make_async_copy(dq_held, dq_out, load_sem.at[0])
+    leave.start()
+    backward_keys(0, 0)
+    own = parts[0] + (1.0 - on_one) * back_in[1].astype(F32) + got_all(home4)
+    parts[0] = own
+    for k in range(BACK):
+        total = parts[0, quarter[k], :] + got(home2[k])
+        dk_out[quarter[k], :] = total[:, 0:128]
+        dv_out[quarter[k], :] = total[:, 128:256]
 
     for copy in cross + [hop4, hop8] + hop6 + [side4, side8] + side2 + side6:
         copy.wait_send()
     for part in range(2):
         for i in range(1, heads):
             stat_copy(part, i).wait_send()
+    leave.wait()
     for group in side_back + [home6, home8, home4, home2]:
         for copy, _, _ in group:
             copy.wait_send()
@@ -402,10 +415,14 @@
     ins, outs, held, sems = refs[0:3], refs[3:6], refs[6:9], refs[9]
     copies = []
     for i in range(3):
-        copies.append((
-            pltpu.make_async_copy(ins[i], held[i], sems.at[0, i]),
-            pltpu.make_async_copy(held[i], outs[i], sems.at[1, i]),
-        ))
+        step = ROWS // 4 if i == 0 else TOK
+        for j in range(ins[i].shape[0] // step):
+            rows = pl.ds(j * step, step)
+            at = len(copies)
+            copies.append((
+                pltpu.make_async_copy(ins[i].at[rows], held[i].at[rows], sems.at[0, at]),
+                pltpu.make_async_copy(held[i].at[rows], outs[i].at[rows], sems.at[1, at]),
+            ))
     for into, _ in copies:
         into.start()
     for into, out in copies:
@@ -431,7 +448,7 @@
                 jax.ShapeDtypeStruct((TOK, HD), F32),
             ),
             in_specs=[any_space] * 8,
-            out_specs=(vmem, vmem, vmem),
+            out_specs=(any_space, vmem, vmem),
             scratch_shapes=[
                 pltpu.SMEM((2,), jnp.int32),
                 pltpu.VMEM((1, 512), F32),
@@ -446,13 +463,14 @@
                 pltpu.VMEM((512, 128), BF16),
                 pltpu.VMEM((2, 8, 128), F32),
                 pltpu.VMEM((2, heads, 8, 128), F32),
-                pltpu.VMEM((2, ROWS, 128), BF16),
-                pltpu.VMEM((2, ROWS, 512), BF16),
+                pltpu.VMEM((ROWS, 128), BF16),
+                pltpu.VMEM((ROWS, 512), BF16),
                 pltpu.VMEM((9, TOK, 256), F32),
                 pltpu.VMEM((8, TOK, 256), BF16),
                 pltpu.VMEM((8, TOK, 256), BF16),
+                pltpu.VMEM((ROWS, HD), F32),
                 sems((8,)), sems((4 * CHUNKS + 4,)), sems((4 * CHUNKS + 4,)),
-                sems((2 * heads,)), sems((2 * heads,)), sems((12,)), sems((12,)),
+                sems((2 * heads,)), sems((2 * heads,)), sems((2 * BACK + 8,)), sems((2 * BACK + 8,)),
             ],
             compiler_params=pltpu.CompilerParams(
                 collective_id=0, has_side_effects=True, vmem_limit_bytes=60 * 1024 * 1024
@@ -468,7 +486,7 @@
             out_shape=tuple(jax.ShapeDtypeStruct(x.shape, F32) for x in (dq, dk, dv)),
             in_specs=[any_space] * 3,
             out_specs=(any_space,) * 3,
-            scratch_shapes=[pltpu.VMEM(x.shape, F32) for x in (dq, dk, dv)] + [sems((2, 3))],
+            scratch_shapes=[pltpu.VMEM(x.shape, F32) for x in (dq, dk, dv)] + [sems((2, 6))],
         )(dq, dk, dv)
         return dq.reshape(TOK, 4, HD), dk.reshape(TOK, 1, HD), dv.reshape(TOK, 1, HD)
 

time: 93.9 us -> 86.4 us (0.920)
  the two profiles are of different devices: /device:TPU:9 before, /device:TPU:31 now
where the time goes in v2:
time: 86.4 us; the launch traced here: 86.3 us
  Pallas kernels  85.6 us (99%)
    pallas_call x1, Pallas kernels, body(): pl.pallas_call(functools.partial(kernel, contexts, heads), name='gauss_ne...  83.7 us
    pallas_call x1, Pallas kernels, body(): pl.pallas_call(hand_on, name='hand_on', out_shape=tuple((jax.ShapeDtypeSt...  1.97 us

profile of v2, /device:TPU:31, one launch (start us, length us, event | category | flops | bytes accessed | tf_op | source)
XLA Modules:
  0.0 86.3 jit_solution(5115533667696490005)
XLA Ops:
  0.6 83.7 %gauss_newton.1 = (f32[1024,128]{1,0:T(8,128)}, f32[256,128]{1,0:T(8,128)}, f32[256,128]{1,0:T(8,128)}) custom-call(bf16[1024,128]{1,0:T(8,128)(2,1)} %bitcast.14, bf16[256,128]{1,0:T(8,128)(2,1)} %bitcast.16, bf16[256,128]{1,0:T(8,128)(2,1)} %bitcast.17, bf16[1024,128]{1,0:T(8,128)(2,1)} %bitcast.15, bf16[256,128]{1,0:T(8,128)(2,1)} %bitcast.18, ...), custom_call_target="tpu_custom_call" | custom-call | tf_op jit(solution)/shard_map/gauss_newton/pallas_call | solution.py:442
  84.3 2.0 %hand_on.1 = (f32[1024,128]{1,0:T(8,128)}, f32[256,128]{1,0:T(8,128)}, f32[256,128]{1,0:T(8,128)}) custom-call(f32[1024,128]{1,0:T(8,128)} %get-tuple-element.9.refs_0_, f32[256,128]{1,0:T(8,128)} %get-tuple-element.10.refs_1_, f32[256,128]{1,0:T(8,128)} %get-tuple-element.11.refs_2_), custom_call_target="tpu_custom_call" | custom-call | tf_op jit(solution)/shard_map/hand_on/pallas_call | solution.py:483
